TPU v7x, 128 devices: a whole 4x4x4 slice. The times are simulated.
128 devices in a mesh: occ: 8 (over y, core), vir: 16 (over z, x).
Axes of the slice: x: 4, y: 4, z: 4, core: 2. Of those that a mesh axis runs over, the one named last changes fastest.
Arguments:
- amplitudes: bfloat16 [9216, 16384], P('occ', 'vir'), may hold values from -6 to 6
- integrals: bfloat16 [16, 8, 1024, 1024], P('vir'), may hold values from -0.0625 to 0.0625
- cd_tiles: int32 [16, 8], P('vir'), may hold values from 0 to 15, as said below
- cd_count: int32 [16], P('vir'), may hold values from 1 to 8, as said below
Outputs:
- residual: bfloat16 [9216, 16384], P('occ', 'vir')
Inputs may be any that keep to these rules, and one draw needn't show every extreme that they name: `cd_tiles`: entries of one row are distinct and the first is the row's own pair tile. `cd_count`: slots at or past the count are unused.
All inputs are finite; a program needn't handle non-finite values.
Results may differ from a plain program's by a relative error of at most 0.0075.
Values may be sent and summed in bfloat16 or wider, within the bound.
No kernel may reach another device: no remote copies, remote signals or barrier semaphores. Data moves between devices by JAX's collectives and lax.ppermute only.
A program may use at most 128 MiB of HBM per device.

v0:
```python
import jax
import jax.numpy as jnp
from jax import lax
from jax.sharding import PartitionSpec as P

TW = 32
K = 1024
OCC_DEV = 12
CD_MAX = 8


def swapped(shard, axis, apart):
    return lax.ppermute(shard, axis, [(i, i ^ 1 << apart) for i in range(lax.axis_size(axis))])


def reflect_rows(matrix):
    occ_devices = lax.axis_size("occ")
    reshaped = matrix.reshape(OCC_DEV, occ_devices, OCC_DEV, matrix.shape[1])
    arrived = lax.all_to_all(reshaped, "occ", split_axis=1, concat_axis=1, tiled=True)
    return arrived.transpose(2, 1, 0, 3).reshape(matrix.shape)


def reflect_tiles(matrix):
    arrived = swapped(matrix, "vir", 0)
    row_count = matrix.shape[0]
    return arrived.reshape(row_count, TW, TW).transpose(0, 2, 1).reshape(row_count, K)


def on_device(amplitudes, integrals, cd_tiles, cd_count):
    row_count = amplitudes.shape[0]
    listed = cd_tiles[0]
    live_count = cd_count[0]
    blocks = integrals[0]
    zero_block = jnp.zeros((row_count, K), jnp.float32)

    def product(col_tile, slot_index):
        int_block = lax.dynamic_index_in_dim(blocks, slot_index, 0, keepdims=False)
        return lax.dot_general(
            col_tile, int_block, (((1,), (1,)), ((), ())), preferred_element_type=jnp.float32
        )

    gathered = lax.all_gather(amplitudes, "vir", axis=1, tiled=True)

    def visit_slot(slot_pos, running):
        tile_id = listed[slot_pos]

        def apply_block(current):
            col_tile = lax.dynamic_slice_in_dim(gathered, tile_id * K, K, 1)
            return current + product(col_tile, slot_pos)

        return lax.cond(slot_pos < live_count, apply_block, lambda current: current, running)

    ladder = lax.fori_loop(0, CD_MAX, visit_slot, zero_block)
    ladder = ladder.astype(jnp.bfloat16)
    mirrored = reflect_tiles(reflect_rows(ladder))
    summed = ladder.astype(jnp.float32) + mirrored.astype(jnp.float32)
    return summed.astype(jnp.bfloat16)


def solution(mesh):
    placed = (P("occ", "vir"), P("vir", None, None, None), P("vir", None), P("vir"))
    return jax.shard_map(
        on_device, mesh=mesh, in_specs=placed, out_specs=P("occ", "vir"), check_vma=False
    )
```

profile of v0, /device:TPU:6, one launch (start us, length us, event | category | flops | bytes accessed | tf_op | source)
XLA Modules:
  0.0 456.2 jit_solution(4664653060656685572)
XLA Ops:
  7.3 223.1 %all-gather.2.cloned.1.call-done = bf16[1152,16384]{1,0:T(8,128)(2,1)} async-done(((bf16[1152,1024]{1,0:T(8,128)(2,1)}), bf16[1152,16384]{1,0:T(8,128)(2,1)}) %all-gather.2.cloned.1.call-update) | async-done | bytes 37748752 | tf_op jit(solution)/shard_map/all_gather | solution.py:42
  233.1 83.6 %while.16 = (s32[]{:T(128)}, f32[1152,1024]{1,0:T(8,128)}, s32[]{:T(128)}, s32[8]{0:T(128)S(1)}, bf16[1152,16384]{1,0:T(8,128)(2,1)}, /*index=5*/bf16[8,1024,1024]{2,1,0:T(8,128)(2,1)}, s32[]{:T(128)}) while((s32[]{:T(128)}, f32[1152,1024]{1,0:T(8,128)}, s32[]{:T(128)}, s32[8]{0:T(128)S(1)}, bf16[1152,16384]{1,0:T(8,128)(2,1)}, ...), condition=%wide.region_3.4_spmd, body=%wide.region_0.3_spmd.sunk | while | flops 2417098752 | bytes 13893871 | solution.py:53
  233.8 9.8 %conditional.2 = (f32[1152,1024]{1,0:T(8,128)}) conditional(s32[]{:T(128)} %convert_element_type.41, f32[1152,1024]{1,0:T(8,128)} %get-tuple-element.236, (s32[]{:T(128)}, s32[8]{0:T(128)S(1)}, bf16[1152,16384]{1,0:T(8,128)(2,1)}, bf16[8,1024,1024]{2,1,0:T(8,128)(2,1)}, f32[1152,1024]{1,0:T(8,128)}) %tuple.45), branch_computations={%region_1.0_spmd, %region_2.2_spmd} | conditional | flops 2417098752 | bytes 13893740 | solution.py:51
  235.1 8.5 %convolution_add_fusion = f32[1152,1024]{1,0:T(8,128)} fusion(f32[1152,1024]{1,0:T(8,128)} %get-tuple-element.165, bf16[1152,16384]{1,0:T(8,128)(2,1)} %get-tuple-element.166, s32[]{:T(128)S(6)} %select_n.19, bf16[8,1024,1024]{2,1,0:T(8,128)(2,1)} %get-tuple-element.169, s32[]{:T(128)S(6)} %select_n.18), kind=kOutput, calls=%fused_computation | convolution fusion | flops 2417098752 | bytes 13893640 | tf_op jit(solution)/shard_map/while/body/eval_jaxpr/cond/branch_1_fun/dot_general | solution.py:38
  244.2 9.8 %conditional.2 = (f32[1152,1024]{1,0:T(8,128)}) conditional(s32[]{:T(128)} %convert_element_type.41, f32[1152,1024]{1,0:T(8,128)} %get-tuple-element.236, (s32[]{:T(128)}, s32[8]{0:T(128)S(1)}, bf16[1152,16384]{1,0:T(8,128)(2,1)}, bf16[8,1024,1024]{2,1,0:T(8,128)(2,1)}, f32[1152,1024]{1,0:T(8,128)}) %tuple.45), branch_computations={%region_1.0_spmd, %region_2.2_spmd} | conditional | flops 2417098752 | bytes 13893740 | solution.py:51
  245.5 8.5 %convolution_add_fusion = f32[1152,1024]{1,0:T(8,128)} fusion(f32[1152,1024]{1,0:T(8,128)} %get-tuple-element.165, bf16[1152,16384]{1,0:T(8,128)(2,1)} %get-tuple-element.166, s32[]{:T(128)S(6)} %select_n.19, bf16[8,1024,1024]{2,1,0:T(8,128)(2,1)} %get-tuple-element.169, s32[]{:T(128)S(6)} %select_n.18), kind=kOutput, calls=%fused_computation | convolution fusion | flops 2417098752 | bytes 13893640 | tf_op jit(solution)/shard_map/while/body/eval_jaxpr/cond/branch_1_fun/dot_general | solution.py:38
  254.7 9.8 %conditional.2 = (f32[1152,1024]{1,0:T(8,128)}) conditional(s32[]{:T(128)} %convert_element_type.41, f32[1152,1024]{1,0:T(8,128)} %get-tuple-element.236, (s32[]{:T(128)}, s32[8]{0:T(128)S(1)}, bf16[1152,16384]{1,0:T(8,128)(2,1)}, bf16[8,1024,1024]{2,1,0:T(8,128)(2,1)}, f32[1152,1024]{1,0:T(8,128)}) %tuple.45), branch_computations={%region_1.0_spmd, %region_2.2_spmd} | conditional | flops 2417098752 | bytes 13893740 | solution.py:51
  256.0 8.5 %convolution_add_fusion = f32[1152,1024]{1,0:T(8,128)} fusion(f32[1152,1024]{1,0:T(8,128)} %get-tuple-element.165, bf16[1152,16384]{1,0:T(8,128)(2,1)} %get-tuple-element.166, s32[]{:T(128)S(6)} %select_n.19, bf16[8,1024,1024]{2,1,0:T(8,128)(2,1)} %get-tuple-element.169, s32[]{:T(128)S(6)} %select_n.18), kind=kOutput, calls=%fused_computation | convolution fusion | flops 2417098752 | bytes 13893640 | tf_op jit(solution)/shard_map/while/body/eval_jaxpr/cond/branch_1_fun/dot_general | solution.py:38
  265.1 9.8 %conditional.2 = (f32[1152,1024]{1,0:T(8,128)}) conditional(s32[]{:T(128)} %convert_element_type.41, f32[1152,1024]{1,0:T(8,128)} %get-tuple-element.236, (s32[]{:T(128)}, s32[8]{0:T(128)S(1)}, bf16[1152,16384]{1,0:T(8,128)(2,1)}, bf16[8,1024,1024]{2,1,0:T(8,128)(2,1)}, f32[1152,1024]{1,0:T(8,128)}) %tuple.45), branch_computations={%region_1.0_spmd, %region_2.2_spmd} | conditional | flops 2417098752 | bytes 13893740 | solution.py:51
  266.4 8.5 %convolution_add_fusion = f32[1152,1024]{1,0:T(8,128)} fusion(f32[1152,1024]{1,0:T(8,128)} %get-tuple-element.165, bf16[1152,16384]{1,0:T(8,128)(2,1)} %get-tuple-element.166, s32[]{:T(128)S(6)} %select_n.19, bf16[8,1024,1024]{2,1,0:T(8,128)(2,1)} %get-tuple-element.169, s32[]{:T(128)S(6)} %select_n.18), kind=kOutput, calls=%fused_computation | convolution fusion | flops 2417098752 | bytes 13893640 | tf_op jit(solution)/shard_map/while/body/eval_jaxpr/cond/branch_1_fun/dot_general | solution.py:38
  275.6 9.8 %conditional.2 = (f32[1152,1024]{1,0:T(8,128)}) conditional(s32[]{:T(128)} %convert_element_type.41, f32[1152,1024]{1,0:T(8,128)} %get-tuple-element.236, (s32[]{:T(128)}, s32[8]{0:T(128)S(1)}, bf16[1152,16384]{1,0:T(8,128)(2,1)}, bf16[8,1024,1024]{2,1,0:T(8,128)(2,1)}, f32[1152,1024]{1,0:T(8,128)}) %tuple.45), branch_computations={%region_1.0_spmd, %region_2.2_spmd} | conditional | flops 2417098752 | bytes 13893740 | solution.py:51
  276.8 8.5 %convolution_add_fusion = f32[1152,1024]{1,0:T(8,128)} fusion(f32[1152,1024]{1,0:T(8,128)} %get-tuple-element.165, bf16[1152,16384]{1,0:T(8,128)(2,1)} %get-tuple-element.166, s32[]{:T(128)S(6)} %select_n.19, bf16[8,1024,1024]{2,1,0:T(8,128)(2,1)} %get-tuple-element.169, s32[]{:T(128)S(6)} %select_n.18), kind=kOutput, calls=%fused_computation | convolution fusion | flops 2417098752 | bytes 13893640 | tf_op jit(solution)/shard_map/while/body/eval_jaxpr/cond/branch_1_fun/dot_general | solution.py:38
  286.0 9.8 %conditional.2 = (f32[1152,1024]{1,0:T(8,128)}) conditional(s32[]{:T(128)} %convert_element_type.41, f32[1152,1024]{1,0:T(8,128)} %get-tuple-element.236, (s32[]{:T(128)}, s32[8]{0:T(128)S(1)}, bf16[1152,16384]{1,0:T(8,128)(2,1)}, bf16[8,1024,1024]{2,1,0:T(8,128)(2,1)}, f32[1152,1024]{1,0:T(8,128)}) %tuple.45), branch_computations={%region_1.0_spmd, %region_2.2_spmd} | conditional | flops 2417098752 | bytes 13893740 | solution.py:51
  287.3 8.5 %convolution_add_fusion = f32[1152,1024]{1,0:T(8,128)} fusion(f32[1152,1024]{1,0:T(8,128)} %get-tuple-element.165, bf16[1152,16384]{1,0:T(8,128)(2,1)} %get-tuple-element.166, s32[]{:T(128)S(6)} %select_n.19, bf16[8,1024,1024]{2,1,0:T(8,128)(2,1)} %get-tuple-element.169, s32[]{:T(128)S(6)} %select_n.18), kind=kOutput, calls=%fused_computation | convolution fusion | flops 2417098752 | bytes 13893640 | tf_op jit(solution)/shard_map/while/body/eval_jaxpr/cond/branch_1_fun/dot_general | solution.py:38
  296.5 9.8 %conditional.2 = (f32[1152,1024]{1,0:T(8,128)}) conditional(s32[]{:T(128)} %convert_element_type.41, f32[1152,1024]{1,0:T(8,128)} %get-tuple-element.236, (s32[]{:T(128)}, s32[8]{0:T(128)S(1)}, bf16[1152,16384]{1,0:T(8,128)(2,1)}, bf16[8,1024,1024]{2,1,0:T(8,128)(2,1)}, f32[1152,1024]{1,0:T(8,128)}) %tuple.45), branch_computations={%region_1.0_spmd, %region_2.2_spmd} | conditional | flops 2417098752 | bytes 13893740 | solution.py:51
  297.7 8.5 %convolution_add_fusion = f32[1152,1024]{1,0:T(8,128)} fusion(f32[1152,1024]{1,0:T(8,128)} %get-tuple-element.165, bf16[1152,16384]{1,0:T(8,128)(2,1)} %get-tuple-element.166, s32[]{:T(128)S(6)} %select_n.19, bf16[8,1024,1024]{2,1,0:T(8,128)(2,1)} %get-tuple-element.169, s32[]{:T(128)S(6)} %select_n.18), kind=kOutput, calls=%fused_computation | convolution fusion | flops 2417098752 | bytes 13893640 | tf_op jit(solution)/shard_map/while/body/eval_jaxpr/cond/branch_1_fun/dot_general | solution.py:38
  306.9 9.8 %conditional.2 = (f32[1152,1024]{1,0:T(8,128)}) conditional(s32[]{:T(128)} %convert_element_type.41, f32[1152,1024]{1,0:T(8,128)} %get-tuple-element.236, (s32[]{:T(128)}, s32[8]{0:T(128)S(1)}, bf16[1152,16384]{1,0:T(8,128)(2,1)}, bf16[8,1024,1024]{2,1,0:T(8,128)(2,1)}, f32[1152,1024]{1,0:T(8,128)}) %tuple.45), branch_computations={%region_1.0_spmd, %region_2.2_spmd} | conditional | flops 2417098752 | bytes 13893740 | solution.py:51
  308.2 8.5 %convolution_add_fusion = f32[1152,1024]{1,0:T(8,128)} fusion(f32[1152,1024]{1,0:T(8,128)} %get-tuple-element.165, bf16[1152,16384]{1,0:T(8,128)(2,1)} %get-tuple-element.166, s32[]{:T(128)S(6)} %select_n.19, bf16[8,1024,1024]{2,1,0:T(8,128)(2,1)} %get-tuple-element.169, s32[]{:T(128)S(6)} %select_n.18), kind=kOutput, calls=%fused_computation | convolution fusion | flops 2417098752 | bytes 13893640 | tf_op jit(solution)/shard_map/while/body/eval_jaxpr/cond/branch_1_fun/dot_general | solution.py:38
  322.8 4.8 %reshape.14 = bf16[12,8,12,1024]{3,2,1,0:T(8,128)(2,1)} reshape(bf16[1152,1024]{1,0:T(8,128)(2,1)} %copy.12) | data formatting | bytes 4718592 | tf_op jit(solution)/shard_map/reshape | solution.py:18
  330.1 42.5 %all_to_all.5 = bf16[12,8,12,1024]{3,2,0,1:T(8,128)(2,1)S(1)} all-to-all(bf16[12,8,12,1024]{3,2,0,1:T(8,128)(2,1)S(1)} %copy.13), channel_id=1, replica_groups=mesh['occ'=8,'vir'=16] {'occ'}, dimensions={1} | all-to-all | bytes 4718592 | tf_op jit(solution)/shard_map/all_to_all | solution.py:19
  375.6 4.9 %reshape.15 = bf16[1152,1024]{1,0:T(8,128)(2,1)} reshape(bf16[12,8,12,1024]{3,2,1,0:T(8,128)(2,1)} %copy.14) | data formatting | bytes 4718592 | tf_op jit(solution)/shard_map/reshape | solution.py:20
  380.5 52.9 %collective-permute-done = bf16[1152,1024]{1,0:T(8,128)(2,1)} collective-permute-done((bf16[1152,1024]{1,0:T(8,128)(2,1)}, bf16[1152,1024]{1,0:T(8,128)(2,1)}, u32[]{:S(2)}, u32[]{:S(2)}) %collective-permute-start) | collective-permute-done | bytes 2359328 | tf_op jit(solution)/shard_map/ppermute | solution.py:13
  433.4 4.6 copy.15
  438.0 5.1 %copy.16 = f32[1152,32,32]{0,2,1:T(8,128)S(1)} copy(f32[1152,32,32]{0,1,2:T(8,128)} %bitcast.15) | data formatting | bytes 9437184 | tf_op jit(solution)/shard_map/convert_element_type | solution.py:56
  (20 shorter events, 26.1 us)
Async XLA Ops:
  6.5 226.6 %copy-start = (s32[1,8]{1,0:T(1,128)S(1)}, s32[1,8]{1,0:T(1,128)}, u32[]{:S(2)}) copy-start(s32[1,8]{1,0:T(1,128)} %param.10) | copy-start | bytes 100
  6.5 223.8 %all-gather.2.cloned.1.call-start = ((), (), s32[]{:S(2)}) async-start(), calls=%async_computation.1 | async-start | bytes 40108032 | tf_op jit(solution)/shard_map/all_gather | solution.py:42
  380.5 52.9 %collective-permute-start = (bf16[1152,1024]{1,0:T(8,128)(2,1)}, bf16[1152,1024]{1,0:T(8,128)(2,1)}, u32[]{:S(2)}, u32[]{:S(2)}) collective-permute-start(bf16[1152,1024]{1,0:T(8,128)(2,1)} %reshape.15), channel_id=1, source_target_pairs={{0,1},{1,0},{2,3},{3,2},{4,5},{5,4},{6,7},{7,6},{8,9},{9,8},{10,11... | collective-permute-start | bytes 7077896 | tf_op jit(solution)/shard_map/ppermute | solution.py:13
Sparse Core Ops, SparseCore 0:
  9.5 220.8 all-gather.1
where the time goes:
time: 457 us; the launch traced here: 456 us
  waiting for transfers between devices  277 us (61%)
  matrix products  68.2 us (15%)
  local copies, waits for them, and re-layouts  42.8 us (9%)
  blocking collectives  42.5 us (9%)
  between operations  13.4 us (3%)
  loops' own time  10.5 us (2%)
    all_gather x1, waiting for transfers between devices, on_device(): gathered = lax.all_gather(amplitudes, 'vir', axis=1, tiled=True)  223 us
    dot_general x8, matrix products, product(): lax.dot_general(col_tile, int_block, (((1,), (1,)), ((), ())), preferred_...  68.2 us
    ppermute x1, waiting for transfers between devices, swapped(): lax.ppermute(shard, axis, [(i, i ^ 1 << apart) for i in range(lax.axis_si...  52.9 us
    all_to_all x1, blocking collectives, reflect_rows(): lax.all_to_all(reshaped, 'occ', split_axis=1, concat_axis=1, tiled=True)  42.5 us
    convert_element_type x2, local copies, waits for them, and re-layouts, on_device(): summed = ladder.astype(jnp.float32) + mirrored.astype(jnp.float32)  9.62 us
  transfers between devices with their start and end apart: 2, of which 2 were waited for; matrix products, arithmetic and copies ran while one was open for 0% of the time, Pallas kernels for 0%

commit v1 on v0

--- a/solution.py
+++ b/solution.py
@@ -16,7 +16,10 @@
 def reflect_rows(matrix):
     occ_devices = lax.axis_size("occ")
     reshaped = matrix.reshape(OCC_DEV, occ_devices, OCC_DEV, matrix.shape[1])
-    arrived = lax.all_to_all(reshaped, "occ", split_axis=1, concat_axis=1, tiled=True)
+    arrived = jnp.concatenate(
+        lax.all_to_all(jnp.stack(jnp.split(reshaped, lax.axis_size("occ"), axis=1)), "occ", 0, 0),
+        axis=1,
+    )
     return arrived.transpose(2, 1, 0, 3).reshape(matrix.shape)
 
 

time: 457 us -> 463 us (1.013)
  local copies, waits for them, and re-layouts: 42.8 us -> 48.5 us
    unnamed x2 -> x9, local copies, waits for them, and re-layouts: 0.01 us -> 7.2 us
where the time goes in v1:
time: 463 us; the launch traced here: 462 us
  waiting for transfers between devices  277 us (60%)
  matrix products  68.2 us (15%)
  local copies, waits for them, and re-layouts  48.5 us (10%)
  blocking collectives  42.5 us (9%)
  between operations  13.5 us (3%)
  loops' own time  10.5 us (2%)
    all_gather x1, waiting for transfers between devices, on_device(): gathered = lax.all_gather(amplitudes, 'vir', axis=1, tiled=True)  223 us
    dot_general x8, matrix products, product(): lax.dot_general(col_tile, int_block, (((1,), (1,)), ((), ())), preferred_...  68.2 us
    ppermute x1, waiting for transfers between devices, swapped(): lax.ppermute(shard, axis, [(i, i ^ 1 << apart) for i in range(lax.axis_si...  52.9 us
    all_to_all x1, blocking collectives, reflect_rows(): lax.all_to_all(jnp.stack(jnp.split(reshaped, lax.axis_size('occ'), axis=1...  42.5 us
    convert_element_type x2, local copies, waits for them, and re-layouts, on_device(): summed = ladder.astype(jnp.float32) + mirrored.astype(jnp.float32)  9.62 us
  transfers between devices with their start and end apart: 2, of which 2 were waited for; matrix products, arithmetic and copies ran while one was open for 0% of the time, Pallas kernels for 0%

profile of v1, /device:TPU:6, one launch (start us, length us, event | category | flops | bytes accessed | tf_op | source)
XLA Modules:
  0.0 462.0 jit_solution(18114048472407707891)
XLA Ops:
  7.3 223.1 %all-gather.2.cloned.1.call-done = bf16[1152,16384]{1,0:T(8,128)(2,1)} async-done(((bf16[1152,1024]{1,0:T(8,128)(2,1)}), bf16[1152,16384]{1,0:T(8,128)(2,1)}) %all-gather.2.cloned.1.call-update) | async-done | bytes 37748752 | tf_op jit(solution)/shard_map/all_gather | solution.py:45
  233.1 83.6 %while.16 = (s32[]{:T(128)}, f32[1152,1024]{1,0:T(8,128)}, s32[]{:T(128)}, s32[8]{0:T(128)S(1)}, bf16[1152,16384]{1,0:T(8,128)(2,1)}, /*index=5*/bf16[8,1024,1024]{2,1,0:T(8,128)(2,1)}, s32[]{:T(128)}) while((s32[]{:T(128)}, f32[1152,1024]{1,0:T(8,128)}, s32[]{:T(128)}, s32[8]{0:T(128)S(1)}, bf16[1152,16384]{1,0:T(8,128)(2,1)}, ...), condition=%wide.region_3.4_spmd, body=%wide.region_0.3_spmd.sunk | while | flops 2417098752 | bytes 13893871 | solution.py:56
  233.8 9.8 %conditional.2 = (f32[1152,1024]{1,0:T(8,128)}) conditional(s32[]{:T(128)} %convert_element_type.41, f32[1152,1024]{1,0:T(8,128)} %get-tuple-element.236, (s32[]{:T(128)}, s32[8]{0:T(128)S(1)}, bf16[1152,16384]{1,0:T(8,128)(2,1)}, bf16[8,1024,1024]{2,1,0:T(8,128)(2,1)}, f32[1152,1024]{1,0:T(8,128)}) %tuple.45), branch_computations={%region_1.0_spmd, %region_2.2_spmd} | conditional | flops 2417098752 | bytes 13893740 | solution.py:54
  235.1 8.5 %convolution_add_fusion = f32[1152,1024]{1,0:T(8,128)} fusion(f32[1152,1024]{1,0:T(8,128)} %get-tuple-element.165, bf16[1152,16384]{1,0:T(8,128)(2,1)} %get-tuple-element.166, s32[]{:T(128)S(6)} %select_n.19, bf16[8,1024,1024]{2,1,0:T(8,128)(2,1)} %get-tuple-element.169, s32[]{:T(128)S(6)} %select_n.18), kind=kOutput, calls=%fused_computation | convolution fusion | flops 2417098752 | bytes 13893640 | tf_op jit(solution)/shard_map/while/body/eval_jaxpr/cond/branch_1_fun/dot_general | solution.py:41
  244.2 9.8 %conditional.2 = (f32[1152,1024]{1,0:T(8,128)}) conditional(s32[]{:T(128)} %convert_element_type.41, f32[1152,1024]{1,0:T(8,128)} %get-tuple-element.236, (s32[]{:T(128)}, s32[8]{0:T(128)S(1)}, bf16[1152,16384]{1,0:T(8,128)(2,1)}, bf16[8,1024,1024]{2,1,0:T(8,128)(2,1)}, f32[1152,1024]{1,0:T(8,128)}) %tuple.45), branch_computations={%region_1.0_spmd, %region_2.2_spmd} | conditional | flops 2417098752 | bytes 13893740 | solution.py:54
  245.5 8.5 %convolution_add_fusion = f32[1152,1024]{1,0:T(8,128)} fusion(f32[1152,1024]{1,0:T(8,128)} %get-tuple-element.165, bf16[1152,16384]{1,0:T(8,128)(2,1)} %get-tuple-element.166, s32[]{:T(128)S(6)} %select_n.19, bf16[8,1024,1024]{2,1,0:T(8,128)(2,1)} %get-tuple-element.169, s32[]{:T(128)S(6)} %select_n.18), kind=kOutput, calls=%fused_computation | convolution fusion | flops 2417098752 | bytes 13893640 | tf_op jit(solution)/shard_map/while/body/eval_jaxpr/cond/branch_1_fun/dot_general | solution.py:41
  254.7 9.8 %conditional.2 = (f32[1152,1024]{1,0:T(8,128)}) conditional(s32[]{:T(128)} %convert_element_type.41, f32[1152,1024]{1,0:T(8,128)} %get-tuple-element.236, (s32[]{:T(128)}, s32[8]{0:T(128)S(1)}, bf16[1152,16384]{1,0:T(8,128)(2,1)}, bf16[8,1024,1024]{2,1,0:T(8,128)(2,1)}, f32[1152,1024]{1,0:T(8,128)}) %tuple.45), branch_computations={%region_1.0_spmd, %region_2.2_spmd} | conditional | flops 2417098752 | bytes 13893740 | solution.py:54
  256.0 8.5 %convolution_add_fusion = f32[1152,1024]{1,0:T(8,128)} fusion(f32[1152,1024]{1,0:T(8,128)} %get-tuple-element.165, bf16[1152,16384]{1,0:T(8,128)(2,1)} %get-tuple-element.166, s32[]{:T(128)S(6)} %select_n.19, bf16[8,1024,1024]{2,1,0:T(8,128)(2,1)} %get-tuple-element.169, s32[]{:T(128)S(6)} %select_n.18), kind=kOutput, calls=%fused_computation | convolution fusion | flops 2417098752 | bytes 13893640 | tf_op jit(solution)/shard_map/while/body/eval_jaxpr/cond/branch_1_fun/dot_general | solution.py:41
  265.1 9.8 %conditional.2 = (f32[1152,1024]{1,0:T(8,128)}) conditional(s32[]{:T(128)} %convert_element_type.41, f32[1152,1024]{1,0:T(8,128)} %get-tuple-element.236, (s32[]{:T(128)}, s32[8]{0:T(128)S(1)}, bf16[1152,16384]{1,0:T(8,128)(2,1)}, bf16[8,1024,1024]{2,1,0:T(8,128)(2,1)}, f32[1152,1024]{1,0:T(8,128)}) %tuple.45), branch_computations={%region_1.0_spmd, %region_2.2_spmd} | conditional | flops 2417098752 | bytes 13893740 | solution.py:54
  266.4 8.5 %convolution_add_fusion = f32[1152,1024]{1,0:T(8,128)} fusion(f32[1152,1024]{1,0:T(8,128)} %get-tuple-element.165, bf16[1152,16384]{1,0:T(8,128)(2,1)} %get-tuple-element.166, s32[]{:T(128)S(6)} %select_n.19, bf16[8,1024,1024]{2,1,0:T(8,128)(2,1)} %get-tuple-element.169, s32[]{:T(128)S(6)} %select_n.18), kind=kOutput, calls=%fused_computation | convolution fusion | flops 2417098752 | bytes 13893640 | tf_op jit(solution)/shard_map/while/body/eval_jaxpr/cond/branch_1_fun/dot_general | solution.py:41
  275.6 9.8 %conditional.2 = (f32[1152,1024]{1,0:T(8,128)}) conditional(s32[]{:T(128)} %convert_element_type.41, f32[1152,1024]{1,0:T(8,128)} %get-tuple-element.236, (s32[]{:T(128)}, s32[8]{0:T(128)S(1)}, bf16[1152,16384]{1,0:T(8,128)(2,1)}, bf16[8,1024,1024]{2,1,0:T(8,128)(2,1)}, f32[1152,1024]{1,0:T(8,128)}) %tuple.45), branch_computations={%region_1.0_spmd, %region_2.2_spmd} | conditional | flops 2417098752 | bytes 13893740 | solution.py:54
  276.8 8.5 %convolution_add_fusion = f32[1152,1024]{1,0:T(8,128)} fusion(f32[1152,1024]{1,0:T(8,128)} %get-tuple-element.165, bf16[1152,16384]{1,0:T(8,128)(2,1)} %get-tuple-element.166, s32[]{:T(128)S(6)} %select_n.19, bf16[8,1024,1024]{2,1,0:T(8,128)(2,1)} %get-tuple-element.169, s32[]{:T(128)S(6)} %select_n.18), kind=kOutput, calls=%fused_computation | convolution fusion | flops 2417098752 | bytes 13893640 | tf_op jit(solution)/shard_map/while/body/eval_jaxpr/cond/branch_1_fun/dot_general | solution.py:41
  286.0 9.8 %conditional.2 = (f32[1152,1024]{1,0:T(8,128)}) conditional(s32[]{:T(128)} %convert_element_type.41, f32[1152,1024]{1,0:T(8,128)} %get-tuple-element.236, (s32[]{:T(128)}, s32[8]{0:T(128)S(1)}, bf16[1152,16384]{1,0:T(8,128)(2,1)}, bf16[8,1024,1024]{2,1,0:T(8,128)(2,1)}, f32[1152,1024]{1,0:T(8,128)}) %tuple.45), branch_computations={%region_1.0_spmd, %region_2.2_spmd} | conditional | flops 2417098752 | bytes 13893740 | solution.py:54
  287.3 8.5 %convolution_add_fusion = f32[1152,1024]{1,0:T(8,128)} fusion(f32[1152,1024]{1,0:T(8,128)} %get-tuple-element.165, bf16[1152,16384]{1,0:T(8,128)(2,1)} %get-tuple-element.166, s32[]{:T(128)S(6)} %select_n.19, bf16[8,1024,1024]{2,1,0:T(8,128)(2,1)} %get-tuple-element.169, s32[]{:T(128)S(6)} %select_n.18), kind=kOutput, calls=%fused_computation | convolution fusion | flops 2417098752 | bytes 13893640 | tf_op jit(solution)/shard_map/while/body/eval_jaxpr/cond/branch_1_fun/dot_general | solution.py:41
  296.5 9.8 %conditional.2 = (f32[1152,1024]{1,0:T(8,128)}) conditional(s32[]{:T(128)} %convert_element_type.41, f32[1152,1024]{1,0:T(8,128)} %get-tuple-element.236, (s32[]{:T(128)}, s32[8]{0:T(128)S(1)}, bf16[1152,16384]{1,0:T(8,128)(2,1)}, bf16[8,1024,1024]{2,1,0:T(8,128)(2,1)}, f32[1152,1024]{1,0:T(8,128)}) %tuple.45), branch_computations={%region_1.0_spmd, %region_2.2_spmd} | conditional | flops 2417098752 | bytes 13893740 | solution.py:54
  297.7 8.5 %convolution_add_fusion = f32[1152,1024]{1,0:T(8,128)} fusion(f32[1152,1024]{1,0:T(8,128)} %get-tuple-element.165, bf16[1152,16384]{1,0:T(8,128)(2,1)} %get-tuple-element.166, s32[]{:T(128)S(6)} %select_n.19, bf16[8,1024,1024]{2,1,0:T(8,128)(2,1)} %get-tuple-element.169, s32[]{:T(128)S(6)} %select_n.18), kind=kOutput, calls=%fused_computation | convolution fusion | flops 2417098752 | bytes 13893640 | tf_op jit(solution)/shard_map/while/body/eval_jaxpr/cond/branch_1_fun/dot_general | solution.py:41
  306.9 9.8 %conditional.2 = (f32[1152,1024]{1,0:T(8,128)}) conditional(s32[]{:T(128)} %convert_element_type.41, f32[1152,1024]{1,0:T(8,128)} %get-tuple-element.236, (s32[]{:T(128)}, s32[8]{0:T(128)S(1)}, bf16[1152,16384]{1,0:T(8,128)(2,1)}, bf16[8,1024,1024]{2,1,0:T(8,128)(2,1)}, f32[1152,1024]{1,0:T(8,128)}) %tuple.45), branch_computations={%region_1.0_spmd, %region_2.2_spmd} | conditional | flops 2417098752 | bytes 13893740 | solution.py:54
  308.2 8.5 %convolution_add_fusion = f32[1152,1024]{1,0:T(8,128)} fusion(f32[1152,1024]{1,0:T(8,128)} %get-tuple-element.165, bf16[1152,16384]{1,0:T(8,128)(2,1)} %get-tuple-element.166, s32[]{:T(128)S(6)} %select_n.19, bf16[8,1024,1024]{2,1,0:T(8,128)(2,1)} %get-tuple-element.169, s32[]{:T(128)S(6)} %select_n.18), kind=kOutput, calls=%fused_computation | convolution fusion | flops 2417098752 | bytes 13893640 | tf_op jit(solution)/shard_map/while/body/eval_jaxpr/cond/branch_1_fun/dot_general | solution.py:41
  322.8 4.8 %reshape.20 = bf16[12,8,12,1024]{3,2,1,0:T(8,128)(2,1)} reshape(bf16[1152,1024]{1,0:T(8,128)(2,1)} %copy.13) | data formatting | bytes 4718592 | tf_op jit(solution)/shard_map/reshape | solution.py:18
  335.9 42.5 %all_to_all.5 = bf16[8,12,1,12,1024]{4,3,1,2,0:T(8,128)(2,1)S(1)} all-to-all(bf16[8,12,1,12,1024]{4,3,1,2,0:T(8,128)(2,1)S(1)} %fusion.5), channel_id=1, replica_groups=mesh['occ'=8,'vir'=16] {'occ'}, dimensions={0} | all-to-all | bytes 4718592 | tf_op jit(solution)/shard_map/all_to_all | solution.py:20
  381.4 4.9 %reshape.23 = bf16[1152,1024]{1,0:T(8,128)(2,1)} reshape(bf16[12,8,12,1024]{3,2,1,0:T(8,128)(2,1)} %copy.21) | data formatting | bytes 4718592 | tf_op jit(solution)/shard_map/reshape | solution.py:23
  386.3 52.9 %collective-permute-done = bf16[1152,1024]{1,0:T(8,128)(2,1)} collective-permute-done((bf16[1152,1024]{1,0:T(8,128)(2,1)}, bf16[1152,1024]{1,0:T(8,128)(2,1)}, u32[]{:S(2)}, u32[]{:S(2)}) %collective-permute-start) | collective-permute-done | bytes 2359328 | tf_op jit(solution)/shard_map/ppermute | solution.py:13
  439.3 4.6 copy.22
  443.8 5.1 %copy.23 = f32[1152,32,32]{0,2,1:T(8,128)S(1)} copy(f32[1152,32,32]{0,1,2:T(8,128)} %bitcast.65) | data formatting | bytes 9437184 | tf_op jit(solution)/shard_map/convert_element_type | solution.py:59
  (27 shorter events, 31.9 us)
Async XLA Ops:
  6.5 226.6 %copy-start = (s32[1,8]{1,0:T(1,128)S(1)}, s32[1,8]{1,0:T(1,128)}, u32[]{:S(2)}) copy-start(s32[1,8]{1,0:T(1,128)} %param.10) | copy-start | bytes 100
  6.5 223.8 %all-gather.2.cloned.1.call-start = ((), (), s32[]{:S(2)}) async-start(), calls=%async_computation.1 | async-start | bytes 40108032 | tf_op jit(solution)/shard_map/all_gather | solution.py:45
  386.3 52.9 %collective-permute-start = (bf16[1152,1024]{1,0:T(8,128)(2,1)}, bf16[1152,1024]{1,0:T(8,128)(2,1)}, u32[]{:S(2)}, u32[]{:S(2)}) collective-permute-start(bf16[1152,1024]{1,0:T(8,128)(2,1)} %reshape.23), channel_id=1, source_target_pairs={{0,1},{1,0},{2,3},{3,2},{4,5},{5,4},{6,7},{7,6},{8,9},{9,8},{10,11... | collective-permute-start | bytes 7077896 | tf_op jit(solution)/shard_map/ppermute | solution.py:13
Sparse Core Ops, SparseCore 0:
  9.5 220.8 all-gather.1
